TPU v7x, 256 devices: a whole 4x4x8 slice. The times are simulated.
256 devices in a mesh: rep: 16 (over y, x), fsdp: 16 (over z, core).
Axes of the slice: x: 4, y: 4, z: 8, core: 2. Of those that a mesh axis runs over, the one named last changes fastest.
Arguments:
- hidden_acts: bfloat16 [16, 8192, 512], P('rep', 'fsdp'), may hold values from -6 to 6
- out_grads: bfloat16 [16, 8192, 8192], P('rep', 'fsdp'), may hold values from -0.15625 to 0.15625
- anchor: float32 [512, 8192], P('fsdp'), may hold values from -6 to 6
- drift: float32 [16, 512, 8192], P('rep', 'fsdp'), may hold values from -120 to 120, as said below
- adam_first: float32 [16, 512, 8192], P('rep', 'fsdp'), may hold values from -6 to 6
- adam_second: float32 [16, 512, 8192], P('rep', 'fsdp'), may hold values from 0.3 to 3
- outer_momentum: float32 [512, 8192], P('fsdp'), may hold values from -6 to 6
Outputs:
- new_first: float32 [16, 512, 8192], P('rep', 'fsdp')
- new_second: float32 [16, 512, 8192], P('rep', 'fsdp')
- new_momentum: float32 [512, 8192], P('fsdp')
- new_anchor: float32 [512, 8192], P('fsdp')
Inputs may be any that keep to these rules, and one draw needn't show every extreme that they name: drift entries are finite reals.
All inputs are finite; a program needn't handle non-finite values.
Results may differ from a plain program's by a relative error of at most 0.0003.
Values sent between devices are 32-bit elements; how exact they have to be, the bound alone decides.
No kernel may reach another device: no remote copies, remote signals or barrier semaphores. Data moves between devices by JAX's collectives and lax.ppermute only.
A program may use at most 128 MiB of HBM per device.

v0:
```python
import math
import jax
import jax.numpy as jnp
from jax import lax
from jax.sharding import PartitionSpec as P

D = 8192
INNER_STEP = 100
beta_first = 0.9
beta_second = 0.95
inner_rate = 0.5
decay_weight = 0.1
outer_rate = 0.7
momentum_coef = 0.9


def outer_update(average, squares, ceiling, momentum_old, anchor_old):
    factor = ceiling / jnp.maximum(jnp.sqrt(squares), ceiling)
    momentum = momentum_coef * momentum_old + factor * average
    updated = anchor_old - outer_rate * (factor * average + momentum_coef * momentum)
    return (momentum, updated)


def per_device(hidden_acts, out_grads, anchor, drift, adam_first, adam_second, outer_momentum):
    activations = hidden_acts[0]
    cotangent = out_grads[0]
    rows_dev = anchor.shape[0]
    gradient = lax.psum_scatter(
        lax.dot_general(
            activations, cotangent, (((0,), (0,)), ((), ())), preferred_element_type=jnp.float32
        ),
        "fsdp",
        scatter_dimension=0,
        tiled=True,
    )
    correction_one = 1.0 - beta_first**INNER_STEP
    correction_two = 1.0 - beta_second**INNER_STEP
    own_drift = drift[0]
    moment_one = beta_first * adam_first[0] + (1.0 - beta_first) * gradient
    moment_two = beta_second * adam_second[0] + (1.0 - beta_second) * gradient * gradient
    update = moment_one / correction_one / (
        jnp.sqrt(moment_two / correction_two) + 1e-08
    ) + decay_weight * (anchor + own_drift)
    pseudo = inner_rate * update - own_drift
    replicas = lax.axis_size("rep")
    ceiling = 0.3 * math.sqrt(rows_dev * lax.axis_size("fsdp") * D)
    average = lax.psum(pseudo, "rep") / replicas
    squares = lax.psum(jnp.sum(average * average), "fsdp")
    momentum, updated = outer_update(average, squares, ceiling, outer_momentum, anchor)
    return (moment_one[None], moment_two[None], momentum, updated)


def solution(mesh):
    return jax.shard_map(
        per_device,
        mesh=mesh,
        in_specs=(
            P("rep", "fsdp", None),
            P("rep", "fsdp", None),
            P("fsdp", None),
            P("rep", "fsdp", None),
            P("rep", "fsdp", None),
            P("rep", "fsdp", None),
            P("fsdp", None),
        ),
        out_specs=(
            P("rep", "fsdp", None),
            P("rep", "fsdp", None),
            P("fsdp", None),
            P("fsdp", None),
        ),
        check_vma=False,
    )
```

profile of v0, /device:TPU:1, one launch (start us, length us, event | category | flops | bytes accessed | tf_op | source)
XLA Modules:
  0.0 261.7 jit_solution(1608500180151418882)
XLA Ops:
  7.2 0.0 copy-start
  7.2 0.0 reduce-scatter.2.cloned.1.call-start
  7.2 1.0 copy-done
  8.2 11.5 %fusion = f32[512,8192]{1,0:T(8,128)} fusion(bf16[1,512,8192]{2,1,0:T(8,128)(2,1)} %param.8, bf16[1,512,512]{2,1,0:T(8,128)(2,1)S(1)} %copy-done), kind=kOutput, calls=%fused_computation | convolution fusion | flops 4294967296 | bytes 25690112 | tf_op jit(solution)/shard_map/dot_general | solution.py:29
  19.7 0.0 copy-start.1
  19.7 0.0 reduce-scatter.2.cloned.1.call-update
  19.7 0.0 copy-start.2
  19.7 0.0 all-reduce.2.cloned.1.call-start
  19.8 103.3 %reduce-scatter.2.cloned.1.call-done = f32[32,8192]{1,0:T(8,128)} async-done(((f32[512,8192]{1,0:T(8,128)}), f32[32,8192]{1,0:T(8,128)}) %reduce-scatter.2.cloned.1.call-update) | async-done | bytes 1048592 | tf_op jit(solution)/shard_map/reduce_scatter | solution.py:28
  123.1 0.0 copy-done.1
  123.1 4.3 %bitcast_subtract_fusion = (f32[32,8192]{1,0:T(8,128)}, f32[1,32,8192]{2,1,0:T(8,128)}, f32[1,32,8192]{2,1,0:T(8,128)}) fusion(f32[1,32,8192]{2,1,0:T(8,128)} %param.10, f32[32,8192]{1,0:T(8,128)S(1)} %copy-done.1, f32[32,8192]{1,0:T(8,128)} %reduce-scatter.2.cloned.1.call-done, f32[1,32,8192]{2,1,0:T(8,128)} %param.11, f32[1,32,8192]{2,1,0:T(8,128)} %param.12), kind=kLoop, calls=%fused_computation.4 | loop fusion | flops 4194304 | bytes 8388608 | tf_op jit(solution)/shard_map/sub | solution.py:44
  127.5 0.0 all-reduce.2.cloned.1.call-update
  127.5 95.5 %all-reduce.2.cloned.1.call-done = f32[32,8192]{1,0:T(8,128)} async-done(((f32[32,8192]{1,0:T(8,128)}), f32[32,8192]{1,0:T(8,128)}) %all-reduce.2.cloned.1.call-update) | async-done | bytes 1048592 | tf_op jit(solution)/shard_map/psum | solution.py:47
  223.0 2.1 multiply_reduce_fusion
  225.1 26.2 %psum.15 = f32[]{:T(128)} all-reduce(f32[]{:T(128)} %multiply_reduce_fusion), channel_id=1, replica_groups=mesh['rep'=16,'fsdp'=16] {'fsdp'}, use_global_device_ids=true, to_apply=%region_3.0 | all-reduce | flops 1 | bytes 8 | tf_op jit(solution)/shard_map/psum | solution.py:48
  252.0 0.0 copy-done.2
  252.0 2.8 %multiply_subtract_fusion = (f32[32,8192]{1,0:T(8,128)}, f32[32,8192]{1,0:T(8,128)}) fusion(f32[32,8192]{1,0:T(8,128)S(1)} %copy-done.1, f32[32,8192]{1,0:T(8,128)} %all-reduce.2.cloned.1.call-done, f32[]{:T(128)S(6)} %mul.75, f32[32,8192]{1,0:T(8,128)S(1)} %copy-done.2), kind=kLoop, calls=%fused_computation.10 | loop fusion | flops 1835008 | bytes 5242884 | tf_op jit(solution)/shard_map/sub | solution.py:20
Async XLA Ops:
  7.2 1.0 copy-start
  7.2 115.9 %reduce-scatter.2.cloned.1.call-start = ((), (), s32[]{:S(2)}) async-start(), calls=%async_computation.1 | async-start | bytes 17825792 | tf_op jit(solution)/shard_map/reduce_scatter | solution.py:28
  19.7 103.4 %copy-start.1 = (f32[32,8192]{1,0:T(8,128)S(1)}, f32[32,8192]{1,0:T(8,128)}, u32[]{:S(2)}) copy-start(f32[32,8192]{1,0:T(8,128)} %param.9) | copy-start | bytes 3145732
  19.7 232.3 %copy-start.2 = (f32[32,8192]{1,0:T(8,128)S(1)}, f32[32,8192]{1,0:T(8,128)}, u32[]{:S(2)}) copy-start(f32[32,8192]{1,0:T(8,128)} %param.13) | copy-start | bytes 3145732
  19.7 203.3 %all-reduce.2.cloned.1.call-start = ((), (), s32[]{:S(2)}) async-start(), calls=%async_computation.2 | async-start | bytes 2097152 | tf_op jit(solution)/shard_map/psum | solution.py:47
Sparse Core Ops, SparseCore 0:
  19.8 103.2 reduce-scatter.1
  127.6 95.3 all-reduce.1
where the time goes:
time: 262 us
  waiting for transfers between devices  199 us (76%)
  blocking collectives  26.2 us (10%)
  between operations  14.8 us (6%)
  matrix products  11.5 us (4%)
  other arithmetic  9.23 us (4%)
    reduce_scatter x1, waiting for transfers between devices, per_device(): lax.psum_scatter(lax.dot_general(activations, cotangent, (((0,), (0,)), (...  103 us
    psum x1, waiting for transfers between devices, per_device(): average = lax.psum(pseudo, 'rep') / replicas  95.5 us
    psum x1, blocking collectives, per_device(): squares = lax.psum(jnp.sum(average * average), 'fsdp')  26.2 us
    dot_general x1, matrix products, per_device(): lax.dot_general(activations, cotangent, (((0,), (0,)), ((), ())), preferr...  11.5 us
  transfers between devices with their start and end apart: 2, of which 2 were waited for; matrix products, arithmetic and copies ran while one was open for 0% of the time, Pallas kernels for 0%

commit v1 on v0

--- a/solution.py
+++ b/solution.py
@@ -44,7 +44,7 @@
     pseudo = inner_rate * update - own_drift
     replicas = lax.axis_size("rep")
     ceiling = 0.3 * math.sqrt(rows_dev * lax.axis_size("fsdp") * D)
-    average = lax.psum(pseudo, "rep") / replicas
+    average = jnp.sum(lax.all_gather(pseudo, "rep"), axis=0) / replicas
     squares = lax.psum(jnp.sum(average * average), "fsdp")
     momentum, updated = outer_update(average, squares, ceiling, outer_momentum, anchor)
     return (moment_one[None], moment_two[None], momentum, updated)

time: 262 us -> 288 us (1.099)
  waiting for transfers between devices: 199 us -> 219 us
  other arithmetic: 9.23 us -> 14.3 us
    all_gather x0 -> x1, waiting for transfers between devices: none -> 116 us  [per_device(): average = jnp.sum(lax.all_gather(pseudo, 'rep'), axis=0) / replicas]
    psum x1 -> x0, waiting for transfers between devices: 95.5 us -> none  [per_device(): average = lax.psum(pseudo, 'rep') / replicas]
    reduce_sum x0 -> x1, other arithmetic: none -> 6.66 us  [per_device(): average = jnp.sum(lax.all_gather(pseudo, 'rep'), axis=0) / replicas]
where the time goes in v1:
time: 288 us; the launch traced here: 286 us
  waiting for transfers between devices  219 us (76%)
  blocking collectives  24.7 us (9%)
  between operations  14.8 us (5%)
  other arithmetic  14.3 us (5%)
  matrix products  11.5 us (4%)
    all_gather x1, waiting for transfers between devices, per_device(): average = jnp.sum(lax.all_gather(pseudo, 'rep'), axis=0) / replicas  116 us
    reduce_scatter x1, waiting for transfers between devices, per_device(): lax.psum_scatter(lax.dot_general(activations, cotangent, (((0,), (0,)), (...  103 us
    psum x1, blocking collectives, per_device(): squares = lax.psum(jnp.sum(average * average), 'fsdp')  24.7 us
    dot_general x1, matrix products, per_device(): lax.dot_general(activations, cotangent, (((0,), (0,)), ((), ())), preferr...  11.5 us
    reduce_sum x1, other arithmetic, per_device(): average = jnp.sum(lax.all_gather(pseudo, 'rep'), axis=0) / replicas  6.66 us
  transfers between devices with their start and end apart: 2, of which 2 were waited for; matrix products, arithmetic and copies ran while one was open for 0% of the time, Pallas kernels for 0%

profile of v1, /device:TPU:1, one launch (start us, length us, event | category | flops | bytes accessed | tf_op | source)
XLA Modules:
  0.0 285.9 jit_solution(11861633441816778142)
XLA Ops:
  7.2 0.0 copy-start
  7.2 0.0 reduce-scatter.2.cloned.1.call-start
  7.2 1.0 copy-done
  8.2 11.5 %fusion = f32[512,8192]{1,0:T(8,128)} fusion(bf16[1,512,8192]{2,1,0:T(8,128)(2,1)} %param.8, bf16[1,512,512]{2,1,0:T(8,128)(2,1)S(1)} %copy-done), kind=kOutput, calls=%fused_computation | convolution fusion | flops 4294967296 | bytes 25690112 | tf_op jit(solution)/shard_map/dot_general | solution.py:29
  19.7 0.0 copy-start.1
  19.7 0.0 copy-start.2
  19.7 0.0 reduce-scatter.2.cloned.1.call-update
  19.7 0.0 all-gather.3.cloned.1.call-start
  19.8 103.3 %reduce-scatter.2.cloned.1.call-done = f32[32,8192]{1,0:T(8,128)} async-done(((f32[512,8192]{1,0:T(8,128)}), f32[32,8192]{1,0:T(8,128)}) %reduce-scatter.2.cloned.1.call-update) | async-done | bytes 1048592 | tf_op jit(solution)/shard_map/reduce_scatter | solution.py:28
  123.1 0.0 copy-done.1
  123.1 0.0 copy-done.2
  123.1 4.0 %bitcast_subtract_fusion = (f32[32,8192]{1,0:T(8,128)}, f32[1,32,8192]{2,1,0:T(8,128)}, f32[1,32,8192]{2,1,0:T(8,128)}) fusion(f32[1,32,8192]{2,1,0:T(8,128)S(1)} %copy-done.2, f32[32,8192]{1,0:T(8,128)S(1)} %copy-done.1, f32[32,8192]{1,0:T(8,128)} %reduce-scatter.2.cloned.1.call-done, f32[1,32,8192]{2,1,0:T(8,128)} %param.11, f32[1,32,8192]{2,1,0:T(8,128)} %param.12), kind=kLoop, calls=%fused_computation.4 | loop fusion | flops 4194304 | bytes 8388608 | tf_op jit(solution)/shard_map/sub | solution.py:44
  127.2 0.0 all-gather.3.cloned.1.call-update
  127.2 116.1 %all-gather.3.cloned.1.call-done = f32[512,8192]{1,0:T(8,128)} async-done(((f32[32,8192]{1,0:T(8,128)}), f32[512,8192]{1,0:T(8,128)}) %all-gather.3.cloned.1.call-update) | async-done | bytes 16777232 | tf_op jit(solution)/shard_map/all_gather | solution.py:47
  243.3 6.7 %reduce_sum.18 = f32[32,8192]{1,0:T(8,128)S(1)} reduce(f32[16,32,8192]{2,1,0:T(8,128)} %bitcast.34, f32[]{:T(128)} %constant.11.clone.1), dimensions={0}, to_apply=%region_1.0 | reduce | flops 3932160 | bytes 17825796 | tf_op jit(solution)/shard_map/reduce_sum | solution.py:47
  250.0 0.9 multiply_reduce_fusion
  250.8 24.7 %psum.7 = f32[]{:T(128)} all-reduce(f32[]{:T(128)} %multiply_reduce_fusion), channel_id=1, replica_groups=mesh['rep'=16,'fsdp'=16] {'fsdp'}, use_global_device_ids=true, to_apply=%region_3.0 | all-reduce | flops 1 | bytes 8 | tf_op jit(solution)/shard_map/psum | solution.py:48
  276.3 2.8 multiply_subtract_fusion
Async XLA Ops:
  7.2 1.0 copy-start
  7.2 115.9 %reduce-scatter.2.cloned.1.call-start = ((), (), s32[]{:S(2)}) async-start(), calls=%async_computation.1 | async-start | bytes 17825792 | tf_op jit(solution)/shard_map/reduce_scatter | solution.py:28
  19.7 103.4 %copy-start.1 = (f32[32,8192]{1,0:T(8,128)S(1)}, f32[32,8192]{1,0:T(8,128)}, u32[]{:S(2)}) copy-start(f32[32,8192]{1,0:T(8,128)} %param.9) | copy-start | bytes 3145732
  19.7 103.4 %copy-start.2 = (f32[1,32,8192]{2,1,0:T(8,128)S(1)}, f32[1,32,8192]{2,1,0:T(8,128)}, u32[]{:S(2)}) copy-start(f32[1,32,8192]{2,1,0:T(8,128)} %param.10) | copy-start | bytes 3145732
  19.7 223.6 %all-gather.3.cloned.1.call-start = ((), (), s32[]{:S(2)}) async-start(), calls=%async_computation.2 | async-start | bytes 17825792 | tf_op jit(solution)/shard_map/all_gather | solution.py:47
Sparse Core Ops, SparseCore 0:
  19.8 103.2 reduce-scatter.1
  127.3 115.9 all-gather.2
